TPU v7x, 32 devices: a whole 2x2x4 slice. The times are simulated.
32 devices in a mesh: fact: 4 (over z), dim: 8 (over y, x, core).
Axes of the slice: x: 2, y: 2, z: 4, core: 2. Of those that a mesh axis runs over, the one named last changes fastest.
Arguments:
- facts: bfloat16 [4096, 512], P(('fact', 'dim')), may hold values from -6 to 6
- dims: bfloat16 [4096, 512], P(('fact', 'dim')), may hold values from -6 to 6
- tiles: bfloat16 [1024, 128, 128], P(('fact', 'dim')), may hold values from -0.125 to 0.125
- links: int32 [1024, 2], P(('fact', 'dim')), may hold values from 0 to 31, as said below
- link_count: int32 [32], P(('fact', 'dim')), may hold values from 8 to 32, as said below
- block_table: int32 [32], replicated, may hold values from 0 to 2
- w_self: bfloat16 [512, 512], replicated, may hold values from -0.25 to 0.25
- w_tables: bfloat16 [3, 512, 512], replicated, may hold values from -0.25 to 0.25
- cot: bfloat16 [4096, 512], P(('fact', 'dim')), may hold values from -6 to 6
Outputs:
- fact_out: bfloat16 [4096, 512], P(('fact', 'dim'))
- grad_dims: float32 [4096, 512], P(('fact', 'dim'))
- grad_w_self: float32 [512, 512], replicated
- grad_w_tables: float32 [3, 512, 512], replicated
Inputs may be any that keep to these rules, and one draw needn't show every extreme that they name: On device k = f * 8 + d (f, d its fact and dim indices), links[l,0] is a fact block among those of rows f * 128 * 8 to (f + 1) * 128 * 8 - 1, and links[l,1] is a dimension block held by a device with dim index d, i.e. links[l,1] % 8 == d. Slots beyond the device's count hold such indices too and are padding. `link_count`: some device has all 32 slots live and some device exactly 8.
All inputs are finite; a program needn't handle non-finite values.
Results may differ from a plain program's by a relative error of at most 0.017.
Values may be sent and summed in bfloat16 or wider, within the bound.
A program may use at most 64 MiB of HBM per device.

v0:
```python
import math
import jax
import jax.numpy as jnp
from jax import lax
from jax.sharding import PartitionSpec as P


def project_rows(rows, row_table, w_tables):
    acc = jnp.zeros((rows.shape[0], w_tables.shape[2]), jnp.float32)
    for table in range(w_tables.shape[0]):
        term = jnp.dot(rows, w_tables[table], preferred_element_type=jnp.float32)
        acc = acc + jnp.where(row_table[:, None] == table, term, jnp.float32(0.0))
    return acc.astype(jnp.bfloat16)


def lookup_tables(global_blocks, block_table):
    every = jnp.arange(block_table.shape[0], dtype=jnp.int32)
    match = global_blocks[:, None] == every[None, :]
    return jnp.sum(jnp.where(match, block_table[None, :], 0), axis=1)


def body(facts, dims, tiles, links, link_count, block_table, w_self, w_tables, cot):
    n_fact = lax.axis_size("fact")
    n_dim = lax.axis_size("dim")
    fact_pos = lax.axis_index("fact")
    dim_pos = lax.axis_index("dim")
    block = tiles.shape[1]
    width = facts.shape[1]
    rows_own = facts.shape[0]
    dim_own = dims.shape[0]
    link_slots = tiles.shape[0]
    tables = w_tables.shape[0]
    shard_rows = rows_own * n_dim
    panel_rows = dim_own * n_fact
    per_owner = dim_own // block
    own_blocks = (fact_pos * n_dim + dim_pos) * per_owner + jnp.arange(per_owner, dtype=jnp.int32)
    own_row_table = jnp.repeat(lookup_tables(own_blocks, block_table), block)
    panel_local = jnp.arange(n_fact * per_owner, dtype=jnp.int32)
    panel_blocks_global = (
        panel_local // per_owner * n_dim + dim_pos
    ) * per_owner + panel_local % per_owner
    panel_row_table = jnp.repeat(lookup_tables(panel_blocks_global, block_table), block)
    panel = project_rows(
        lax.all_gather(dims, "fact", axis=0, tiled=True), panel_row_table, w_tables
    )
    fact_blk = links[:, 0] - fact_pos * (shard_rows // block)
    global_dim = links[:, 1]
    holder = global_dim // per_owner // n_dim
    dim_blk = holder * per_owner + global_dim % per_owner
    live = (jnp.arange(link_slots, dtype=jnp.int32) < link_count[0]).astype(jnp.float32)
    group = math.gcd(link_slots, 32)
    steps_count = link_slots // group
    tile_groups = tiles.reshape(steps_count, group, block, block)
    fact_groups = fact_blk.reshape(steps_count, group)
    dim_groups = dim_blk.reshape(steps_count, group)
    live_groups = live.reshape(steps_count, group)
    panel_blocks = panel.reshape(panel_rows // block, block, width)

    def forward_step(acc, xs):
        tile, fact_ids, dim_ids, alive = xs
        contrib = jnp.einsum(
            "lij,ljd->lid", tile, panel_blocks[dim_ids], preferred_element_type=jnp.float32
        )
        return (acc.at[fact_ids].add(contrib * alive[:, None, None]), None)

    start_fwd = jnp.zeros((shard_rows // block, block, width), jnp.float32)
    partial_value, _ = lax.scan(
        forward_step, start_fwd, (tile_groups, fact_groups, dim_groups, live_groups)
    )
    agg = lax.psum_scatter(
        partial_value.reshape(shard_rows, width).astype(jnp.bfloat16),
        "dim",
        scatter_dimension=0,
        tiled=True,
    ).astype(jnp.float32)
    pre = jnp.dot(facts, w_self, preferred_element_type=jnp.float32) + agg
    fact_out = jax.nn.silu(pre).astype(jnp.bfloat16)
    sig = jax.nn.sigmoid(pre)
    grad_pre = (cot.astype(jnp.float32) * sig * (1.0 + pre * (1.0 - sig))).astype(jnp.bfloat16)
    total_facts = rows_own * n_fact * n_dim
    total_dims = dim_own * n_fact * n_dim
    grad_self = lax.dot_general(
        facts, grad_pre, (((0,), (0,)), ((), ())), preferred_element_type=jnp.float32
    ) * total_facts ** (-0.5)
    shard_grad = lax.all_gather(grad_pre, "dim", axis=0, tiled=True)
    grad_blocks = shard_grad.reshape(shard_rows // block, block, width)

    def backward_step(acc, xs):
        tile, fact_ids, dim_ids, alive = xs
        contrib = jnp.einsum(
            "lji,ljd->lid", tile, grad_blocks[fact_ids], preferred_element_type=jnp.float32
        )
        return (acc.at[dim_ids].add(contrib * alive[:, None, None]), None)

    start_bwd = jnp.zeros((panel_rows // block, block, width), jnp.float32)
    panel_grad, _ = lax.scan(
        backward_step, start_bwd, (tile_groups, fact_groups, dim_groups, live_groups)
    )
    own_grad = lax.psum_scatter(
        panel_grad.reshape(panel_rows, width).astype(jnp.bfloat16),
        "fact",
        scatter_dimension=0,
        tiled=True,
    )
    grad_dims = jnp.zeros((dim_own, width), jnp.float32)
    table_grads = []
    for table in range(tables):
        term = lax.dot_general(
            own_grad, w_tables[table], (((1,), (1,)), ((), ())), preferred_element_type=jnp.float32
        )
        grad_dims = grad_dims + jnp.where(own_row_table[:, None] == table, term, jnp.float32(0.0))
        masked = jnp.where(own_row_table[:, None] == table, dims, jnp.zeros_like(dims))
        table_grads.append(
            lax.dot_general(
                masked, own_grad, (((0,), (0,)), ((), ())), preferred_element_type=jnp.float32
            )
            * total_dims ** (-0.5)
        )
    grad_tab = jnp.stack(table_grads)
    grad_self, grad_tab = lax.psum((grad_self, grad_tab), ("fact", "dim"))
    return (fact_out, grad_dims, grad_self, grad_tab)


def solution(mesh):
    placed = (
        P(("fact", "dim"), None),
        P(("fact", "dim"), None),
        P(("fact", "dim"), None, None),
        P(("fact", "dim"), None),
        P(("fact", "dim")),
        P(),
        P(),
        P(),
        P(("fact", "dim"), None),
    )
    return jax.shard_map(
        body,
        mesh=mesh,
        in_specs=placed,
        out_specs=(P(("fact", "dim"), None), P(("fact", "dim"), None), P(), P()),
        check_vma=False,
    )
```

profile of v0, /device:TPU:0, one launch (start us, length us, event | category | flops | bytes accessed | tf_op | source)
XLA Modules:
  0.0 342.8 jit_solution(11924869971505833211)
XLA Ops:
  7.2 0.0 copy-start
  7.2 0.0 copy-start.7
  7.2 0.0 reduce-scatter.3.cloned.1.call-start
  7.3 0.9 select_reduce_fusion
  8.2 17.6 %all_gather.6 = bf16[512,512]{1,0:T(8,128)(2,1)S(1)} all-gather(bf16[128,512]{1,0:T(8,128)(2,1)} %param.10), channel_id=1, replica_groups=mesh['fact'=4,'dim'=8] {'fact'}, dimensions={0}, use_global_device_ids=true | all-gather | bytes 655360 | tf_op jit(solution)/shard_map/all_gather | solution.py:44
  25.8 0.1 broadcast_bitcast_fusion
  25.8 1.5 convolution_select_fusion
  27.3 2.5 convolution_select_fusion.1
  29.8 0.1 broadcast_bitcast_fusion.2
  29.8 0.0 copy-done.7
  30.5 1.8 fusion.6
  32.4 2.8 gather_fusion
  35.2 0.0 copy-done
  35.2 7.1 %multiply_bitcast_fusion.1 = f32[32,128,512]{1,2,0:T(8,128)} fusion(f32[32]{0:T(128)S(1)} %compare_convert_fusion, bf16[32,128,512]{2,1,0:T(8,128)(2,1)} %gather_fusion, bf16[32,128,128]{2,1,0:T(8,128)(2,1)S(1)} %copy-done), kind=kOutput, calls=%fused_computation.5 | convolution fusion | flops 538968064 | bytes 13631616 | tf_op jit(solution)/shard_map/while/body/eval_jaxpr/lij,ljd->lid/dot_general | solution.py:61
  42.2 9.0 %copy.22 = f32[32,128,512]{2,1,0:T(8,128)} copy(f32[32,128,512]{1,2,0:T(8,128)} %multiply_bitcast_fusion.1) | data formatting | bytes 16777216 | tf_op jit(solution)/shard_map/while/body/eval_jaxpr/mul | solution.py:64
  51.2 0.2 broadcast_in_dim.107
  51.5 11.8 %scatter_fusion = f32[8,128,512]{2,1,0:T(8,128)S(1)} fusion(f32[8,128,512]{2,1,0:T(8,128)S(1)} %broadcast_in_dim.107, s32[32]{0:T(128)S(1)} %get-tuple-element.63, f32[32,128,512]{2,1,0:T(8,128)} %copy.22), kind=kCustom, calls=%fused_computation.2 | custom fusion | flops 2097152 | bytes 25165952 | tf_op jit(solution)/shard_map/while/body/eval_jaxpr/scatter-add | solution.py:64
  63.3 0.0 copy-start.6
  63.3 0.0 copy-start.8
  63.3 1.1 convert_element_type.32
  64.4 0.0 reduce-scatter.3.cloned.1.call-update
  64.4 0.0 all-gather.2.cloned.1.call-start
  64.5 37.8 %reduce-scatter.3.cloned.1.call-done = bf16[128,512]{1,0:T(8,128)(2,1)} async-done(((bf16[1024,512]{1,0:T(8,128)(2,1)}), bf16[128,512]{1,0:T(8,128)(2,1)}) %reduce-scatter.3.cloned.1.call-update) | async-done | bytes 131088 | tf_op jit(solution)/shard_map/reduce_scatter | solution.py:70
  102.3 0.0 copy-done.6
  102.3 0.0 copy-done.8
  102.3 2.1 multiply_convert_fusion
  104.4 0.0 all-gather.2.cloned.1.call-update
  104.4 0.0 reduce-scatter.5.cloned.1.call-start
  104.5 23.7 %all-gather.2.cloned.1.call-done = bf16[1024,512]{1,0:T(8,128)(2,1)} async-done(((bf16[128,512]{1,0:T(8,128)(2,1)}), bf16[1024,512]{1,0:T(8,128)(2,1)}) %all-gather.2.cloned.1.call-update) | async-done | bytes 1048592 | tf_op jit(solution)/shard_map/all_gather | solution.py:85
  128.2 4.0 %gather_fusion.1 = bf16[32,128,512]{2,1,0:T(8,128)(2,1)} fusion(bf16[8,128,512]{2,1,0:T(8,128)(2,1)} %bitcast.61, s32[1024]{0:T(1024)S(1)} %pad_clamp_fusion), kind=kCustom, calls=%fused_computation.1 | custom fusion | bytes 8388736 | tf_op jit(solution)/shard_map/while/body/eval_jaxpr/gather | solution.py:91
  132.2 7.1 %multiply_bitcast_fusion = f32[32,128,512]{1,2,0:T(8,128)} fusion(f32[32]{0:T(128)S(1)} %compare_convert_fusion, bf16[32,128,512]{2,1,0:T(8,128)(2,1)} %gather_fusion.1, bf16[32,128,128]{2,1,0:T(8,128)(2,1)S(1)} %copy-done), kind=kOutput, calls=%fused_computation.4 | convolution fusion | flops 538968064 | bytes 13631616 | tf_op jit(solution)/shard_map/while/body/eval_jaxpr/lji,ljd->lid/dot_general | solution.py:90
  139.2 9.0 %copy.24 = f32[32,128,512]{2,1,0:T(8,128)} copy(f32[32,128,512]{1,2,0:T(8,128)} %multiply_bitcast_fusion) | data formatting | bytes 16777216 | tf_op jit(solution)/shard_map/while/body/eval_jaxpr/mul | solution.py:93
  148.2 0.1 broadcast_in_dim.119
  148.4 0.0 copy-start.9
  148.4 0.0 copy-start.5
  148.4 0.0 copy-start.4
  148.4 11.7 %scatter_fusion.1 = f32[4,128,512]{2,1,0:T(8,128)S(1)} fusion(f32[4,128,512]{2,1,0:T(8,128)S(1)} %broadcast_in_dim.119, s32[32]{0:T(128)S(1)} %get-tuple-element.62, f32[32,128,512]{2,1,0:T(8,128)} %copy.24), kind=kCustom, calls=%fused_computation.3 | custom fusion | flops 2097152 | bytes 25165952 | tf_op jit(solution)/shard_map/while/body/eval_jaxpr/scatter-add | solution.py:93
  160.1 0.9 convert_element_type.38
  160.9 0.0 reduce-scatter.5.cloned.1.call-update
  160.9 0.0 all-reduce.3.cloned.1.call-start
  161.0 0.0 copy-done.9
  161.0 0.6 fusion.30
  163.6 0.0 copy-done.5
  163.6 1.3 fusion.3
  164.9 18.1 %reduce-scatter.5.cloned.1.call-done = bf16[128,512]{1,0:T(8,128)(2,1)} async-done(((bf16[512,512]{1,0:T(8,128)(2,1)}), bf16[128,512]{1,0:T(8,128)(2,1)}) %reduce-scatter.5.cloned.1.call-update) | async-done | bytes 131088 | tf_op jit(solution)/shard_map/reduce_scatter | solution.py:99
  183.0 0.0 copy-done.4
  183.0 1.2 fusion
  184.2 1.2 fusion.1
  185.4 1.2 fusion.2
  186.7 0.0 copy-start.2
  186.7 0.0 copy-start.3
  186.7 2.0 pad_maximum_fusion
  188.7 0.0 all-reduce.3.cloned.1.call-update
  188.7 0.0 copy-done.2
  188.7 0.0 copy-done.3
  188.7 0.3 convolution_select_fusion.4
  189.0 0.3 fusion.7
  189.3 1.0 fusion.8
  190.3 139.5 %all-reduce.3.cloned.1.call-done = (f32[512,512]{0,1:T(8,128)}, f32[3,512,512]{2,1,0:T(8,128)}) async-done(((f32[512,512]{0,1:T(8,128)}, f32[3,512,512]{2,1,0:T(8,128)}), (f32[512,512]{0,1:T(8,128)}, f32[3,512,512]{2,1,0:T(8,128)})) %all-reduce.3.cloned.1.call-update) | async-done | bytes 4194320 | tf_op jit(solution)/shard_map/psum | solution.py:120
  329.8 0.0 copy-start.1
  329.8 2.6 copy.25
  332.4 3.9 %copy.33 = f32[3,512,512]{2,1,0:T(8,128)} copy(f32[3,512,512]{2,1,0:T(8,128)} %get-tuple-element.72) | data formatting | bytes 6291456
  336.3 0.0 copy-done.1
  (6 shorter events, 0.0 us)
Async XLA Ops:
  7.2 28.0 %copy-start = (bf16[32,128,128]{2,1,0:T(8,128)(2,1)S(1)}, bf16[32,128,128]{2,1,0:T(8,128)(2,1)}, u32[]{:S(2)}) copy-start(bf16[32,128,128]{2,1,0:T(8,128)(2,1)} %param.11) | copy-start | bytes 3145732
  7.2 22.7 %copy-start.7 = (s32[32,2]{0,1:T(2,128)S(1)}, s32[32,2]{0,1:T(2,128)}, u32[]{:S(2)}) copy-start(s32[32,2]{0,1:T(2,128)} %param.12) | copy-start | bytes 772
  7.2 95.1 %reduce-scatter.3.cloned.1.call-start = ((), (), s32[]{:S(2)}) async-start(), calls=%async_computation.2 | async-start | bytes 1179648 | tf_op jit(solution)/shard_map/reduce_scatter | solution.py:70
  63.3 39.0 %copy-start.6 = (bf16[128,512]{1,0:T(8,128)(2,1)S(1)}, bf16[128,512]{1,0:T(8,128)(2,1)}, u32[]{:S(2)}) copy-start(bf16[128,512]{1,0:T(8,128)(2,1)} %param.9) | copy-start | bytes 393220
  63.3 39.0 %copy-start.8 = (bf16[128,512]{1,0:T(8,128)(2,1)S(1)}, bf16[128,512]{1,0:T(8,128)(2,1)}, u32[]{:S(2)}) copy-start(bf16[128,512]{1,0:T(8,128)(2,1)} %param.17) | copy-start | bytes 393220
  64.4 63.7 %all-gather.2.cloned.1.call-start = ((), (), s32[]{:S(2)}) async-start(), calls=%async_computation.3 | async-start | bytes 1179648 | tf_op jit(solution)/shard_map/all_gather | solution.py:85
  104.4 78.5 %reduce-scatter.5.cloned.1.call-start = ((), (), s32[]{:S(2)}) async-start(), calls=%async_computation.4 | async-start | bytes 655360 | tf_op jit(solution)/shard_map/reduce_scatter | solution.py:99
  148.4 12.6 %copy-start.9 = (s32[32]{0:T(128)S(1)}, s32[32]{0:T(128)}, u32[]{:S(2)}) copy-start(s32[32]{0:T(128)} %param.14) | copy-start | bytes 388
  148.4 15.2 %copy-start.5 = (bf16[128,512]{1,0:T(8,128)(2,1)S(1)}, bf16[128,512]{1,0:T(8,128)(2,1)}, u32[]{:S(2)}) copy-start(bf16[128,512]{1,0:T(8,128)(2,1)} %get-tuple-element.60) | copy-start | bytes 393220
  148.4 34.6 %copy-start.4 = (bf16[128,512]{1,0:T(8,128)(2,1)S(1)}, bf16[128,512]{1,0:T(8,128)(2,1)}, u32[]{:S(2)}) copy-start(bf16[128,512]{1,0:T(8,128)(2,1)} %param.10) | copy-start | bytes 393220
  160.9 168.9 %all-reduce.3.cloned.1.call-start = ((), (), s32[]{:S(2)}) async-start(), calls=%async_computation.5 | async-start | bytes 8388608 | tf_op jit(solution)/shard_map/psum | solution.py:120
  186.7 2.0 copy-start.2
  186.7 2.0 copy-start.3
  329.8 6.5 %copy-start.1 = (bf16[32,128,128]{2,1,0:T(8,128)(2,1)S(1)}, bf16[32,128,128]{2,1,0:T(8,128)(2,1)}, u32[]{:S(2)}) copy-start(bf16[32,128,128]{2,1,0:T(8,128)(2,1)} %param.11) | copy-start | bytes 3145732
Sparse Core Ops, SparseCore 0:
  64.5 37.7 reduce-scatter.2
  104.8 23.3 all-gather.1
  161.1 21.8 reduce-scatter.4
  189.1 140.6 all-reduce.2
where the time goes:
time: 344 us; the launch traced here: 343 us
  waiting for transfers between devices  219 us (64%)
  local copies, waits for them, and re-layouts  31.8 us (9%)
  other arithmetic  29 us (8%)
  matrix products  28.6 us (8%)
  blocking collectives  17.6 us (5%)
  between operations  16.6 us (5%)
    psum x1, waiting for transfers between devices, body(): grad_self, grad_tab = lax.psum((grad_self, grad_tab), ('fact', 'dim'))  139 us
    reduce_scatter x1, waiting for transfers between devices, body(): lax.psum_scatter(partial_value.reshape(shard_rows, width).astype(jnp.bflo...  37.8 us
    all_gather x1, waiting for transfers between devices, body(): shard_grad = lax.all_gather(grad_pre, 'dim', axis=0, tiled=True)  23.7 us
    reduce_scatter x1, waiting for transfers between devices, body(): lax.psum_scatter(panel_grad.reshape(panel_rows, width).astype(jnp.bfloat1...  18.1 us
    all_gather x1, blocking collectives, body(): lax.all_gather(dims, 'fact', axis=0, tiled=True)  17.6 us
    scatter-add x1, other arithmetic, forward_step(): return (acc.at[fact_ids].add(contrib * alive[:, None, None]), None)  11.8 us
    scatter-add x1, other arithmetic, backward_step(): return (acc.at[dim_ids].add(contrib * alive[:, None, None]), None)  11.7 us
    mul x1, local copies, waits for them, and re-layouts, forward_step(): return (acc.at[fact_ids].add(contrib * alive[:, None, None]), None)  9 us
  transfers between devices with their start and end apart: 4, of which 4 were waited for; matrix products, arithmetic and copies ran while one was open for 1% of the time, Pallas kernels for 0%

commit v1 on v0

--- a/solution.py
+++ b/solution.py
@@ -117,7 +117,7 @@
             * total_dims ** (-0.5)
         )
     grad_tab = jnp.stack(table_grads)
-    grad_self, grad_tab = lax.psum((grad_self, grad_tab), ("fact", "dim"))
+    grad_self, grad_tab = lax.psum(lax.psum((grad_self, grad_tab), "dim"), "fact")
     return (fact_out, grad_dims, grad_self, grad_tab)
 
 

time: 344 us -> 439 us (1.28)
  waiting for transfers between devices: 219 us -> 314 us
    psum x1 -> x2, waiting for transfers between devices: 139 us -> 235 us  [the longest x1 156 us: body(): lax.psum(lax.psum((grad_self, grad_tab), 'dim'), 'fact')]
  transfers between devices with their start and end apart: 4 -> 5, of which waited for: 4 -> 5; matrix products, arithmetic and copies ran while one was open for 1% -> 1% of each run, Pallas kernels for 0% -> 0%
where the time goes in v1:
time: 439 us; the launch traced here: 438 us
  waiting for transfers between devices  314 us (72%)
  local copies, waits for them, and re-layouts  31.8 us (7%)
  other arithmetic  29 us (7%)
  matrix products  28.6 us (7%)
  blocking collectives  17.6 us (4%)
  between operations  16.6 us (4%)
    psum x1, waiting for transfers between devices, body(): lax.psum(lax.psum((grad_self, grad_tab), 'dim'), 'fact')  156 us
    psum x1, waiting for transfers between devices, body(): lax.psum((grad_self, grad_tab), 'dim')  79.2 us
    reduce_scatter x1, waiting for transfers between devices, body(): lax.psum_scatter(partial_value.reshape(shard_rows, width).astype(jnp.bflo...  37.8 us
    all_gather x1, waiting for transfers between devices, body(): shard_grad = lax.all_gather(grad_pre, 'dim', axis=0, tiled=True)  23.7 us
    reduce_scatter x1, waiting for transfers between devices, body(): lax.psum_scatter(panel_grad.reshape(panel_rows, width).astype(jnp.bfloat1...  18.1 us
    all_gather x1, blocking collectives, body(): lax.all_gather(dims, 'fact', axis=0, tiled=True)  17.6 us
    scatter-add x1, other arithmetic, forward_step(): return (acc.at[fact_ids].add(contrib * alive[:, None, None]), None)  11.8 us
    scatter-add x1, other arithmetic, backward_step(): return (acc.at[dim_ids].add(contrib * alive[:, None, None]), None)  11.7 us
  transfers between devices with their start and end apart: 5, of which 5 were waited for; matrix products, arithmetic and copies ran while one was open for 1% of the time, Pallas kernels for 0%

profile of v1, /device:TPU:0, one launch (start us, length us, event | category | flops | bytes accessed | tf_op | source)
XLA Modules:
  0.0 438.2 jit_solution(7971238284229240168)
XLA Ops:
  7.2 0.0 copy-start
  7.2 0.0 copy-start.7
  7.2 0.0 reduce-scatter.3.cloned.1.call-start
  7.3 0.9 select_reduce_fusion
  8.2 17.6 %all_gather.6 = bf16[512,512]{1,0:T(8,128)(2,1)S(1)} all-gather(bf16[128,512]{1,0:T(8,128)(2,1)} %param.10), channel_id=1, replica_groups=mesh['fact'=4,'dim'=8] {'fact'}, dimensions={0}, use_global_device_ids=true | all-gather | bytes 655360 | tf_op jit(solution)/shard_map/all_gather | solution.py:44
  25.8 0.1 broadcast_bitcast_fusion
  25.8 1.5 convolution_select_fusion
  27.3 2.5 convolution_select_fusion.1
  29.8 0.1 broadcast_bitcast_fusion.2
  29.8 0.0 copy-done.7
  30.5 1.8 fusion.6
  32.4 2.8 gather_fusion
  35.2 0.0 copy-done
  35.2 7.1 %multiply_bitcast_fusion.1 = f32[32,128,512]{1,2,0:T(8,128)} fusion(f32[32]{0:T(128)S(1)} %compare_convert_fusion, bf16[32,128,512]{2,1,0:T(8,128)(2,1)} %gather_fusion, bf16[32,128,128]{2,1,0:T(8,128)(2,1)S(1)} %copy-done), kind=kOutput, calls=%fused_computation.5 | convolution fusion | flops 538968064 | bytes 13631616 | tf_op jit(solution)/shard_map/while/body/eval_jaxpr/lij,ljd->lid/dot_general | solution.py:61
  42.2 9.0 %copy.22 = f32[32,128,512]{2,1,0:T(8,128)} copy(f32[32,128,512]{1,2,0:T(8,128)} %multiply_bitcast_fusion.1) | data formatting | bytes 16777216 | tf_op jit(solution)/shard_map/while/body/eval_jaxpr/mul | solution.py:64
  51.2 0.2 broadcast_in_dim.107
  51.5 11.8 %scatter_fusion = f32[8,128,512]{2,1,0:T(8,128)S(1)} fusion(f32[8,128,512]{2,1,0:T(8,128)S(1)} %broadcast_in_dim.107, s32[32]{0:T(128)S(1)} %get-tuple-element.65, f32[32,128,512]{2,1,0:T(8,128)} %copy.22), kind=kCustom, calls=%fused_computation.2 | custom fusion | flops 2097152 | bytes 25165952 | tf_op jit(solution)/shard_map/while/body/eval_jaxpr/scatter-add | solution.py:64
  63.3 0.0 copy-start.6
  63.3 0.0 copy-start.8
  63.3 1.1 convert_element_type.32
  64.4 0.0 reduce-scatter.3.cloned.1.call-update
  64.4 0.0 all-gather.2.cloned.1.call-start
  64.5 37.8 %reduce-scatter.3.cloned.1.call-done = bf16[128,512]{1,0:T(8,128)(2,1)} async-done(((bf16[1024,512]{1,0:T(8,128)(2,1)}), bf16[128,512]{1,0:T(8,128)(2,1)}) %reduce-scatter.3.cloned.1.call-update) | async-done | bytes 131088 | tf_op jit(solution)/shard_map/reduce_scatter | solution.py:70
  102.3 0.0 copy-done.6
  102.3 0.0 copy-done.8
  102.3 2.1 multiply_convert_fusion
  104.4 0.0 all-gather.2.cloned.1.call-update
  104.4 0.0 reduce-scatter.5.cloned.1.call-start
  104.5 23.7 %all-gather.2.cloned.1.call-done = bf16[1024,512]{1,0:T(8,128)(2,1)} async-done(((bf16[128,512]{1,0:T(8,128)(2,1)}), bf16[1024,512]{1,0:T(8,128)(2,1)}) %all-gather.2.cloned.1.call-update) | async-done | bytes 1048592 | tf_op jit(solution)/shard_map/all_gather | solution.py:85
  128.2 4.0 gather_fusion.1
  132.2 7.1 %multiply_bitcast_fusion = f32[32,128,512]{1,2,0:T(8,128)} fusion(f32[32]{0:T(128)S(1)} %compare_convert_fusion, bf16[32,128,512]{2,1,0:T(8,128)(2,1)} %gather_fusion.1, bf16[32,128,128]{2,1,0:T(8,128)(2,1)S(1)} %copy-done), kind=kOutput, calls=%fused_computation.4 | convolution fusion | flops 538968064 | bytes 13631616 | tf_op jit(solution)/shard_map/while/body/eval_jaxpr/lji,ljd->lid/dot_general | solution.py:90
  139.2 9.0 %copy.24 = f32[32,128,512]{2,1,0:T(8,128)} copy(f32[32,128,512]{1,2,0:T(8,128)} %multiply_bitcast_fusion) | data formatting | bytes 16777216 | tf_op jit(solution)/shard_map/while/body/eval_jaxpr/mul | solution.py:93
  148.2 0.1 broadcast_in_dim.119
  148.3 0.0 copy-start.9
  148.3 0.0 copy-start.5
  148.4 0.0 copy-start.4
  148.4 11.7 %scatter_fusion.1 = f32[4,128,512]{2,1,0:T(8,128)S(1)} fusion(f32[4,128,512]{2,1,0:T(8,128)S(1)} %broadcast_in_dim.119, s32[32]{0:T(128)S(1)} %get-tuple-element.64, f32[32,128,512]{2,1,0:T(8,128)} %copy.24), kind=kCustom, calls=%fused_computation.3 | custom fusion | flops 2097152 | bytes 25165952 | tf_op jit(solution)/shard_map/while/body/eval_jaxpr/scatter-add | solution.py:93
  160.0 0.9 convert_element_type.38
  160.9 0.0 reduce-scatter.5.cloned.1.call-update
  160.9 0.0 all-reduce.5.cloned.1.call-start
  161.0 0.0 copy-done.9
  161.0 0.6 fusion.30
  163.6 0.0 copy-done.5
  163.6 1.3 fusion.3
  164.9 18.1 %reduce-scatter.5.cloned.1.call-done = bf16[128,512]{1,0:T(8,128)(2,1)} async-done(((bf16[512,512]{1,0:T(8,128)(2,1)}), bf16[128,512]{1,0:T(8,128)(2,1)}) %reduce-scatter.5.cloned.1.call-update) | async-done | bytes 131088 | tf_op jit(solution)/shard_map/reduce_scatter | solution.py:99
  182.9 0.0 copy-done.4
  182.9 1.2 fusion
  184.2 1.2 fusion.1
  185.4 1.2 fusion.2
  186.6 2.0 pad_maximum_fusion
  188.6 0.0 copy-start.2
  188.6 0.0 all-reduce.5.cloned.1.call-update
  188.6 0.0 all-reduce.7.cloned.1.call-start
  188.7 79.2 %all-reduce.5.cloned.1.call-done = (f32[512,512]{0,1:T(8,128)}, f32[3,512,512]{2,1,0:T(8,128)}) async-done(((f32[512,512]{0,1:T(8,128)}, f32[3,512,512]{2,1,0:T(8,128)}), (f32[512,512]{0,1:T(8,128)}, f32[3,512,512]{2,1,0:T(8,128)})) %all-reduce.5.cloned.1.call-update) | async-done | bytes 4194320 | tf_op jit(solution)/shard_map/psum | solution.py:120
  267.8 0.0 all-reduce.7.cloned.1.call-update
  267.9 0.0 copy-done.2
  267.9 0.0 copy-done.3
  267.9 0.3 convolution_select_fusion.4
  268.2 0.3 fusion.7
  268.5 1.0 fusion.8
  269.5 155.7 %all-reduce.7.cloned.1.call-done = (f32[512,512]{0,1:T(8,128)}, f32[3,512,512]{2,1,0:T(8,128)}) async-done(((f32[512,512]{0,1:T(8,128)}, f32[3,512,512]{2,1,0:T(8,128)}), (f32[512,512]{0,1:T(8,128)}, f32[3,512,512]{2,1,0:T(8,128)})) %all-reduce.7.cloned.1.call-update) | async-done | bytes 4194320 | tf_op jit(solution)/shard_map/psum | solution.py:120
  425.2 2.6 copy.25
  427.8 3.9 copy.35
  431.7 0.0 copy-done.1
  (8 shorter events, 0.0 us)
Async XLA Ops:
  7.2 28.0 %copy-start = (bf16[32,128,128]{2,1,0:T(8,128)(2,1)S(1)}, bf16[32,128,128]{2,1,0:T(8,128)(2,1)}, u32[]{:S(2)}) copy-start(bf16[32,128,128]{2,1,0:T(8,128)(2,1)} %param.11) | copy-start | bytes 3145732
  7.2 22.7 %copy-start.7 = (s32[32,2]{0,1:T(2,128)S(1)}, s32[32,2]{0,1:T(2,128)}, u32[]{:S(2)}) copy-start(s32[32,2]{0,1:T(2,128)} %param.12) | copy-start | bytes 772
  7.2 95.1 %reduce-scatter.3.cloned.1.call-start = ((), (), s32[]{:S(2)}) async-start(), calls=%async_computation.2 | async-start | bytes 1179648 | tf_op jit(solution)/shard_map/reduce_scatter | solution.py:70
  63.3 39.0 %copy-start.6 = (bf16[128,512]{1,0:T(8,128)(2,1)S(1)}, bf16[128,512]{1,0:T(8,128)(2,1)}, u32[]{:S(2)}) copy-start(bf16[128,512]{1,0:T(8,128)(2,1)} %param.9) | copy-start | bytes 393220
  63.3 39.0 %copy-start.8 = (bf16[128,512]{1,0:T(8,128)(2,1)S(1)}, bf16[128,512]{1,0:T(8,128)(2,1)}, u32[]{:S(2)}) copy-start(bf16[128,512]{1,0:T(8,128)(2,1)} %param.17) | copy-start | bytes 393220
  64.4 63.7 %all-gather.2.cloned.1.call-start = ((), (), s32[]{:S(2)}) async-start(), calls=%async_computation.3 | async-start | bytes 1179648 | tf_op jit(solution)/shard_map/all_gather | solution.py:85
  104.4 78.5 %reduce-scatter.5.cloned.1.call-start = ((), (), s32[]{:S(2)}) async-start(), calls=%async_computation.4 | async-start | bytes 655360 | tf_op jit(solution)/shard_map/reduce_scatter | solution.py:99
  148.3 12.6 %copy-start.9 = (s32[32]{0:T(128)S(1)}, s32[32]{0:T(128)}, u32[]{:S(2)}) copy-start(s32[32]{0:T(128)} %param.14) | copy-start | bytes 388
  148.3 15.2 %copy-start.5 = (bf16[128,512]{1,0:T(8,128)(2,1)S(1)}, bf16[128,512]{1,0:T(8,128)(2,1)}, u32[]{:S(2)}) copy-start(bf16[128,512]{1,0:T(8,128)(2,1)} %get-tuple-element.62) | copy-start | bytes 393220
  148.4 34.6 %copy-start.4 = (bf16[128,512]{1,0:T(8,128)(2,1)S(1)}, bf16[128,512]{1,0:T(8,128)(2,1)}, u32[]{:S(2)}) copy-start(bf16[128,512]{1,0:T(8,128)(2,1)} %param.10) | copy-start | bytes 393220
  160.9 106.9 %all-reduce.5.cloned.1.call-start = ((), (), s32[]{:S(2)}) async-start(), calls=%async_computation.5 | async-start | bytes 8388608 | tf_op jit(solution)/shard_map/psum | solution.py:120
  188.6 79.3 %copy-start.2 = (bf16[128,512]{1,0:T(8,128)(2,1)S(1)}, bf16[128,512]{1,0:T(8,128)(2,1)}, u32[]{:S(2)}) copy-start(bf16[128,512]{1,0:T(8,128)(2,1)} %reduce-scatter.5.cloned.1.call-done) | copy-start | bytes 393220
  188.6 79.3 %copy-start.3 = (bf16[3,512,512]{2,1,0:T(8,128)(2,1)S(1)}, bf16[3,512,512]{2,1,0:T(8,128)(2,1)}, u32[]{:S(2)}) copy-start(bf16[3,512,512]{2,1,0:T(8,128)(2,1)} %param.16) | copy-start | bytes 4718596
  188.6 236.6 %all-reduce.7.cloned.1.call-start = ((), (), s32[]{:S(2)}) async-start(), calls=%async_computation.6 | async-start | bytes 8388608 | tf_op jit(solution)/shard_map/psum | solution.py:120
  425.2 6.5 %copy-start.1 = (bf16[32,128,128]{2,1,0:T(8,128)(2,1)S(1)}, bf16[32,128,128]{2,1,0:T(8,128)(2,1)}, u32[]{:S(2)}) copy-start(bf16[32,128,128]{2,1,0:T(8,128)(2,1)} %param.11) | copy-start | bytes 3145732
Sparse Core Ops, SparseCore 0:
  64.5 37.7 reduce-scatter.2
  104.8 23.3 all-gather.1
  161.0 21.8 reduce-scatter.4
  188.7 79.0 all-reduce.4
  270.1 155.0 all-reduce.6
